TPU v7x, 32 devices: a whole 2x2x4 slice. The times are simulated.
32 devices in a mesh: fsdp: 4 (over y, x), ctx: 2 (over core), tp: 4 (over z).
Axes of the slice: x: 2, y: 2, z: 4, core: 2. Of those that a mesh axis runs over, the one named last changes fastest.
Arguments:
- block_input: float32 [4, 1024, 2048], P('fsdp', 'ctx'), may hold values from -6 to 6
- cotangent: float32 [4, 1024, 2048], P('fsdp', 'ctx'), may hold values from -6 to 6
- w_query: bfloat16 [2048, 2048], P(('fsdp', 'ctx'), 'tp'), may hold values from -0.125 to 0.125
- w_key: bfloat16 [2048, 512], P(('fsdp', 'ctx'), 'tp'), may hold values from -0.125 to 0.125
- w_value: bfloat16 [2048, 512], P(('fsdp', 'ctx'), 'tp'), may hold values from -0.125 to 0.125
- w_output: bfloat16 [2048, 2048], P('tp', ('fsdp', 'ctx')), may hold values from -4 to 4
- w_gate: bfloat16 [2048, 8192], P(('fsdp', 'ctx'), 'tp'), may hold values from -0.125 to 0.125
- w_up: bfloat16 [2048, 8192], P(('fsdp', 'ctx'), 'tp'), may hold values from -0.125 to 0.125
- w_down: bfloat16 [8192, 2048], P('tp', ('fsdp', 'ctx')), may hold values from -0.0625 to 0.0625
- attn_gain: bfloat16 [2048], P(('fsdp', 'ctx')), may hold values from 0.5 to 1.5
- ffn_gain: bfloat16 [2048], P(('fsdp', 'ctx')), may hold values from 0.5 to 1.5
Outputs:
- block_output: float32 [4, 1024, 2048], P('fsdp', 'ctx')
- input_grad: float32 [4, 1024, 2048], P('fsdp', 'ctx')
- grad_query: float32 [2048, 2048], P(('fsdp', 'ctx'), 'tp')
- grad_key: float32 [2048, 512], P(('fsdp', 'ctx'), 'tp')
- grad_value: float32 [2048, 512], P(('fsdp', 'ctx'), 'tp')
- grad_output: float32 [2048, 2048], P('tp', ('fsdp', 'ctx'))
- grad_gate: float32 [2048, 8192], P(('fsdp', 'ctx'), 'tp')
- grad_up: float32 [2048, 8192], P(('fsdp', 'ctx'), 'tp')
- grad_down: float32 [8192, 2048], P('tp', ('fsdp', 'ctx'))
- grad_attn_gain: float32 [2048], P(('fsdp', 'ctx'))
- grad_ffn_gain: float32 [2048], P(('fsdp', 'ctx'))
All inputs are finite; a program needn't handle non-finite values.
Results may differ from a plain program's by a relative error of at most 0.013.
Values may be sent and summed in bfloat16 or wider, within the bound.
No kernel may reach another device: no remote copies, remote signals or barrier semaphores. Data moves between devices by JAX's collectives and lax.ppermute only.
A program may use at most 256 MiB of HBM per device.

v0:
```python
import jax
import jax.numpy as jnp
from jax import lax
from jax.sharding import PartitionSpec as P

HD = 64
EPS = 1e-05
BASE = 500000.0
NEG = -1e30


def shifted(shard, axis, by):
    count = lax.axis_size(axis)
    pairs = [(i, i + by) for i in range(count) if 0 <= i + by < count]
    return lax.ppermute(shard, axis, pairs)


def rotate(values, positions, sign):
    half = values.shape[-1] // 2
    inverse = BASE ** (-(jnp.arange(half, dtype=jnp.float32) * 2.0) / values.shape[-1])
    angle = positions.astype(jnp.float32)[:, None] * inverse[None, :]
    cosine = jnp.cos(angle)[:, None, :]
    sine = sign * jnp.sin(angle)[:, None, :]
    first = values[..., :half]
    second = values[..., half:]
    return jnp.concatenate(
        [first * cosine - second * sine, second * cosine + first * sine], axis=-1
    )


def norm_forward(rows, gain):
    scale = lax.rsqrt(jnp.mean(rows * rows, axis=-1, keepdims=True) + EPS)
    return (rows * scale * gain, scale)


def norm_backward(rows, scale, gain, grad):
    weighted = grad * gain
    d_rows = scale * weighted - rows * scale**3 * jnp.mean(weighted * rows, axis=-1, keepdims=True)
    return (d_rows, jnp.sum(grad * rows * scale, axis=0))


def forward_block(queries, keys, vals, allow, scale):
    scores = jnp.einsum("gbd,kd->gbk", queries, keys, preferred_element_type=jnp.float32) * scale
    scores = jnp.where(allow[None], scores, NEG)
    top = jnp.max(scores, axis=-1, keepdims=True)
    total = top[..., 0] + jnp.log(jnp.sum(jnp.exp(scores - top), axis=-1))
    probs = jnp.exp(scores - total[..., None]).astype(jnp.bfloat16)
    out = jnp.einsum("gbk,kd->gbd", probs, vals, preferred_element_type=jnp.float32)
    return (out.astype(jnp.bfloat16), total)


def backward_block(queries, keys, vals, allow, total, grad_out, out, scale):
    scores = jnp.einsum("gbd,kd->gbk", queries, keys, preferred_element_type=jnp.float32) * scale
    scores = jnp.where(allow[None], scores, NEG)
    probs = jnp.exp(scores - total[..., None])
    rounded = probs.astype(jnp.bfloat16)
    d_vals = jnp.einsum("gbk,gbd->kd", rounded, grad_out, preferred_element_type=jnp.float32)
    d_probs = jnp.einsum("gbd,kd->gbk", grad_out, vals, preferred_element_type=jnp.float32)
    delta = jnp.sum(grad_out.astype(jnp.float32) * out.astype(jnp.float32), axis=-1)
    d_scores = (probs * (d_probs - delta[..., None]) * scale).astype(jnp.bfloat16)
    d_query = jnp.einsum("gbk,kd->gbd", d_scores, keys, preferred_element_type=jnp.float32)
    d_keys = jnp.einsum("gbk,gbd->kd", d_scores, queries, preferred_element_type=jnp.float32)
    return (d_query, d_keys, d_vals)


def split_blocks(tensor, count, block):
    return tensor.reshape((tensor.shape[0], count, block) + tensor.shape[2:]).swapaxes(0, 1)


def attention_forward(grouped, keys, vals, allow, block, scale):

    def per_head(items):
        head_q, head_k, head_v = items
        groups, rows, width = head_q.shape
        count = rows // block
        outs, totals = lax.map(
            lambda piece: forward_block(piece[0], head_k, head_v, piece[1], scale),
            (split_blocks(head_q, count, block), allow.reshape(count, block, allow.shape[1])),
        )
        return (
            outs.swapaxes(0, 1).reshape(groups, rows, width),
            totals.swapaxes(0, 1).reshape(groups, rows),
        )

    return lax.map(per_head, (grouped, keys, vals))


def attention_backward(grouped, keys, vals, allow, totals, grads, outs, block, scale):

    def per_head(items):
        head_q, head_k, head_v, head_t, head_g, head_o = items
        groups, rows, width = head_q.shape
        count = rows // block

        def step(carry, piece):
            d_query, d_keys, d_vals = backward_block(
                piece[0], head_k, head_v, piece[1], piece[2], piece[3], piece[4], scale
            )
            return ((carry[0] + d_keys, carry[1] + d_vals), d_query)

        zeros = jnp.zeros(head_k.shape, jnp.float32)
        pieces = (
            split_blocks(head_q, count, block),
            allow.reshape(count, block, allow.shape[1]),
            split_blocks(head_t, count, block),
            split_blocks(head_g, count, block),
            split_blocks(head_o, count, block),
        )
        (d_keys, d_vals), d_query = lax.scan(step, (zeros, zeros), pieces)
        return (d_query.swapaxes(0, 1).reshape(groups, rows, width), d_keys, d_vals)

    return lax.map(per_head, (grouped, keys, vals, totals, grads, outs))


def dotf(left, right):
    return jnp.dot(left, right, preferred_element_type=jnp.float32)


def body(
    block_input,
    cotangent,
    w_query,
    w_key,
    w_value,
    w_output,
    w_gate,
    w_up,
    w_down,
    attn_gain,
    ffn_gain,
):
    wq, wk, wv, wo, wg, wu, wd, gain_qa, gain_qf = (
        lax.all_gather(w_query, ("fsdp", "ctx"), axis=0, tiled=True),
        lax.all_gather(w_key, ("fsdp", "ctx"), axis=0, tiled=True),
        lax.all_gather(w_value, ("fsdp", "ctx"), axis=0, tiled=True),
        lax.all_gather(w_output, ("fsdp", "ctx"), axis=1, tiled=True),
        lax.all_gather(w_gate, ("fsdp", "ctx"), axis=0, tiled=True),
        lax.all_gather(w_up, ("fsdp", "ctx"), axis=0, tiled=True),
        lax.all_gather(w_down, ("fsdp", "ctx"), axis=1, tiled=True),
        lax.all_gather(attn_gain, ("fsdp", "ctx"), axis=0, tiled=True),
        lax.all_gather(ffn_gain, ("fsdp", "ctx"), axis=0, tiled=True),
    )
    rows = block_input[0]
    cot = cotangent[0]
    local = rows.shape[0]
    block = min(512, local)
    scale = HD ** (-0.5)
    heads = wq.shape[1] // HD
    kv_heads = wk.shape[1] // HD
    groups = heads // kv_heads
    place = lax.axis_index("ctx")
    positions = place * local + jnp.arange(local, dtype=jnp.int32)
    gain_a = gain_qa.astype(jnp.float32)
    gain_f = gain_qf.astype(jnp.float32)
    normed_f, scale_a = norm_forward(rows, gain_a)
    normed = normed_f.astype(jnp.bfloat16)
    query = dotf(normed, wq).reshape(local, heads, HD)
    keys = dotf(normed, wk).reshape(local, kv_heads, HD)
    vals = dotf(normed, wv)
    query_rot = rotate(query, positions, 1.0).astype(jnp.bfloat16)
    keys_rot = rotate(keys, positions, 1.0).astype(jnp.bfloat16).reshape(local, kv_heads * HD)
    vals_b = vals.astype(jnp.bfloat16)
    keys_prev, vals_prev = shifted((keys_rot, vals_b), "ctx", 1)
    all_keys = (
        jnp.concatenate([keys_prev, keys_rot], axis=0)
        .reshape(2 * local, kv_heads, HD)
        .transpose(1, 0, 2)
    )
    all_vals = (
        jnp.concatenate([vals_prev, vals_b], axis=0)
        .reshape(2 * local, kv_heads, HD)
        .transpose(1, 0, 2)
    )
    grouped = query_rot.reshape(local, kv_heads, groups, HD).transpose(1, 2, 0, 3)
    index = jnp.arange(local, dtype=jnp.int32)
    earlier = jnp.broadcast_to(place > 0, (local, local))
    causal = index[None, :] <= index[:, None]
    allow = jnp.concatenate([earlier, causal], axis=1)
    attn, totals = attention_forward(grouped, all_keys, all_vals, allow, block, scale)
    attn_flat = attn.transpose(2, 0, 1, 3).reshape(local, heads * HD)
    hidden = rows + lax.psum(dotf(attn_flat, wo), "tp")
    hnorm_f, scale_f = norm_forward(hidden, gain_f)
    hnorm = hnorm_f.astype(jnp.bfloat16)
    gate = dotf(hnorm, wg)
    up = dotf(hnorm, wu)
    sigma = jax.nn.sigmoid(gate)
    active = gate * sigma
    inner = (active * up).astype(jnp.bfloat16)
    out = hidden + lax.psum(dotf(inner, wd).astype(jnp.bfloat16), "tp").astype(jnp.float32)
    cot_b = cot.astype(jnp.bfloat16)
    d_inner = dotf(cot_b, wd.T)
    d_gate = (d_inner * up * sigma * (1.0 + gate * (1.0 - sigma))).astype(jnp.bfloat16)
    d_up = (d_inner * active).astype(jnp.bfloat16)
    d_hnorm = lax.psum(dotf(d_gate, wg.T) + dotf(d_up, wu.T), "tp")
    d_norm, g_ffn = norm_backward(hidden, scale_f, gain_f, d_hnorm)
    d_hidden = cot + d_norm
    dh_b = d_hidden.astype(jnp.bfloat16)
    d_attn = (
        dotf(dh_b, wo.T)
        .astype(jnp.bfloat16)
        .reshape(local, kv_heads, groups, HD)
        .transpose(1, 2, 0, 3)
    )
    d_query, d_keys, d_vals = attention_backward(
        grouped, all_keys, all_vals, allow, totals, d_attn, attn, block, scale
    )
    keys_grad = d_keys.transpose(1, 0, 2).reshape(2 * local, kv_heads * HD)
    vals_grad = d_vals.transpose(1, 0, 2).reshape(2 * local, kv_heads * HD)
    keys_back, vals_back = shifted((keys_grad[:local], vals_grad[:local]), "ctx", -1)
    keys_own = keys_grad[local:] + keys_back
    vals_own = vals_grad[local:] + vals_back
    d_query = d_query.transpose(2, 0, 1, 3).reshape(local, heads, HD)
    dq_b = rotate(d_query, positions, -1.0).astype(jnp.bfloat16).reshape(local, heads * HD)
    dk_b = (
        rotate(keys_own.reshape(local, kv_heads, HD), positions, -1.0)
        .astype(jnp.bfloat16)
        .reshape(local, kv_heads * HD)
    )
    dv_b = vals_own.astype(jnp.bfloat16)
    d_normed = lax.psum(dotf(dq_b, wq.T) + dotf(dk_b, wk.T) + dotf(dv_b, wv.T), "tp")
    d_rows, g_attn = norm_backward(rows, scale_a, gain_a, d_normed)
    d_input = d_hidden + d_rows
    s_query, s_key, s_value, s_output, s_gate, s_up, s_down, s_attn, s_ffn = (
        lax.psum_scatter(dotf(normed.T, dq_b), ("fsdp", "ctx"), scatter_dimension=0, tiled=True),
        lax.psum_scatter(dotf(normed.T, dk_b), ("fsdp", "ctx"), scatter_dimension=0, tiled=True),
        lax.psum_scatter(dotf(normed.T, dv_b), ("fsdp", "ctx"), scatter_dimension=0, tiled=True),
        lax.psum_scatter(dotf(attn_flat.T, dh_b), ("fsdp", "ctx"), scatter_dimension=1, tiled=True),
        lax.psum_scatter(dotf(hnorm.T, d_gate), ("fsdp", "ctx"), scatter_dimension=0, tiled=True),
        lax.psum_scatter(dotf(hnorm.T, d_up), ("fsdp", "ctx"), scatter_dimension=0, tiled=True),
        lax.psum_scatter(dotf(inner.T, cot_b), ("fsdp", "ctx"), scatter_dimension=1, tiled=True),
        lax.psum_scatter(g_attn, ("fsdp", "ctx"), scatter_dimension=0, tiled=True),
        lax.psum_scatter(g_ffn, ("fsdp", "ctx"), scatter_dimension=0, tiled=True),
    )
    return (
        out[None],
        d_input[None],
        s_query,
        s_key,
        s_value,
        s_output,
        s_gate,
        s_up,
        s_down,
        s_attn,
        s_ffn,
    )


def solution(mesh):
    placed = (
        P("fsdp", "ctx", None),
        P("fsdp", "ctx", None),
        P(("fsdp", "ctx"), "tp"),
        P(("fsdp", "ctx"), "tp"),
        P(("fsdp", "ctx"), "tp"),
        P("tp", ("fsdp", "ctx")),
        P(("fsdp", "ctx"), "tp"),
        P(("fsdp", "ctx"), "tp"),
        P("tp", ("fsdp", "ctx")),
        P(("fsdp", "ctx")),
        P(("fsdp", "ctx")),
    )
    return jax.shard_map(
        body,
        mesh=mesh,
        in_specs=placed,
        out_specs=(
            P("fsdp", "ctx", None),
            P("fsdp", "ctx", None),
            P(("fsdp", "ctx"), "tp"),
            P(("fsdp", "ctx"), "tp"),
            P(("fsdp", "ctx"), "tp"),
            P("tp", ("fsdp", "ctx")),
            P(("fsdp", "ctx"), "tp"),
            P(("fsdp", "ctx"), "tp"),
            P("tp", ("fsdp", "ctx")),
            P(("fsdp", "ctx")),
            P(("fsdp", "ctx")),
        ),
        check_vma=False,
    )
```

profile of v0, /device:TPU:0, one launch (start us, length us, event | category | flops | bytes accessed | tf_op | source)
XLA Modules:
  0.0 1437.5 jit_solution(5688634115593749319)
XLA Ops:
  8.6 10.4 all-gather
  19.0 10.7 all_gather.29
  30.0 3.0 fusion.52
  36.5 2.9 collective-permute-start
  39.4 8.9 all_gather.30
  51.5 2.9 collective-permute-start.1
  55.7 1.7 pad_maximum_fusion
  57.4 1.8 copy.30
  59.2 3.9 copy.28
  63.2 2.9 fusion.65
  66.3 12.7 while.10
  66.3 1.6 fusion.154
  67.9 2.3 exponential_reduce_fusion.2
  70.3 2.3 fusion.155
  72.6 1.6 fusion.154
  74.3 2.3 exponential_reduce_fusion.2
  76.6 2.3 fusion.155
  79.0 4.0 all-gather.10.cloned.1.call-done
  83.0 4.9 fusion.86
  89.7 9.1 all-gather.1
  98.8 144.2 %all-reduce.9.cloned.1.call-done = f32[512,2048]{1,0:T(8,128)} async-done(((f32[512,2048]{1,0:T(8,128)}), f32[512,2048]{1,0:T(8,128)}) %all-reduce.9.cloned.1.call-update) | async-done | bytes 4194320 | tf_op jit(solution)/shard_map/psum | solution.py:181
  243.0 4.0 multiply_reduce_fusion.2
  247.1 2.0 copy-done.1
  249.1 1.7 multiply_convert_fusion.4
  250.8 47.2 %all-gather.12.cloned.1.call-done = bf16[2048,2048]{1,0:T(8,128)(2,1)} async-done(((bf16[256,2048]{1,0:T(8,128)(2,1)}), bf16[2048,2048]{1,0:T(8,128)(2,1)}) %all-gather.12.cloned.1.call-update) | async-done | bytes 8388624 | tf_op jit(solution)/shard_map/all_gather | solution.py:137
  298.0 10.5 fusion.87
  308.6 45.5 %all-gather.14.cloned.1.call-done = bf16[2048,2048]{1,0:T(8,128)(2,1)} async-done(((bf16[256,2048]{1,0:T(8,128)(2,1)}), bf16[2048,2048]{1,0:T(8,128)(2,1)}) %all-gather.14.cloned.1.call-update) | async-done | bytes 8388624 | tf_op jit(solution)/shard_map/all_gather | solution.py:138
  354.1 10.5 fusion.88
  364.6 47.1 %all-gather.16.cloned.1.call-done = bf16[2048,2048]{1,0:T(8,128)(2,1)} async-done(((bf16[2048,256]{1,0:T(8,128)(2,1)}), bf16[2048,2048]{1,0:T(8,128)(2,1)}) %all-gather.16.cloned.1.call-update) | async-done | bytes 8388624 | tf_op jit(solution)/shard_map/all_gather | solution.py:139
  411.7 15.3 %multiply_convert_fusion.1 = (bf16[512,2048]{1,0:T(8,128)(2,1)S(1)}, bf16[512,2048]{1,0:T(8,128)(2,1)}, bf16[512,2048]{1,0:T(8,128)(2,1)}) fusion(f32[512,2048]{1,0:T(8,128)} %fusion.87, f32[512,2048]{1,0:T(8,128)} %fusion.88, bf16[2048,2048]{1,0:T(8,128)(2,1)} %all-gather.16.cloned.1.call-done, f32[1,512,2048]{2,1,0:T(8,128)} %param.16), kind=kOutput, calls=%fused_computation.79 | convolution fusion | flops 4310695936 | bytes 27262976 | tf_op jit(solution)/shard_map/dot_general | solution.py:116
  427.0 8.4 fusion.89
  435.4 6.1 convolution_add_fusion
  441.6 9.8 convolution_convert_fusion
  451.7 145.0 %all-reduce.13.cloned.1.call-done = f32[512,2048]{1,0:T(8,128)} async-done(((f32[512,2048]{1,0:T(8,128)}), f32[512,2048]{1,0:T(8,128)}) %all-reduce.13.cloned.1.call-update) | async-done | bytes 4194320 | tf_op jit(solution)/shard_map/psum | solution.py:194
  596.7 4.5 multiply_reduce_fusion
  601.2 83.0 %all-reduce.11.cloned.1.call-done = bf16[512,2048]{1,0:T(8,128)(2,1)} async-done(((bf16[512,2048]{1,0:T(8,128)(2,1)}), bf16[512,2048]{1,0:T(8,128)(2,1)}) %all-reduce.11.cloned.1.call-update) | async-done | bytes 2097168 | tf_op jit(solution)/shard_map/psum | solution.py:189
  684.2 8.1 bitcast_add_fusion
  692.3 2.0 copy-done.4
  695.6 20.4 %while.27 = (s32[]{:T(128)}, f32[2,4,512,64]{2,3,1,0:T(8,128)}, f32[2,1024,64]{1,2,0:T(8,128)S(1)}, f32[2,1024,64]{1,2,0:T(8,128)}, pred[512,1024]{1,0:T(8,128)(...) while((s32[]{:T(128)}, f32[2,4,512,64]{2,3,1,0:T(8,128)}, ...), condition=%wide.region_12.13_spmd, body=%wide.region_10.12_spmd.sunk | while | flops 1365768192 | bytes 50255028 | solution.py:112
  697.1 3.3 multiply_convert_fusion.7
  702.8 3.1 fusion.170
  707.3 3.3 multiply_convert_fusion.7
  710.6 1.4 fusion.168
  713.0 3.1 fusion.170
  718.6 1.5 collective-permute-start.2
  724.0 2.8 add_add_fusion
  726.8 3.5 fusion.92
  730.4 1.8 fusion.67
  732.2 5.7 fusion.73
  738.0 3.3 fusion.69
  741.4 1.5 copy-done.11
  742.9 9.7 fusion.93
  752.7 9.9 fusion.94
  764.1 10.4 fusion.82
  776.4 105.3 %all-reduce.15.cloned.1.call-done = f32[512,2048]{1,0:T(8,128)} async-done(((f32[512,2048]{1,0:T(8,128)}), f32[512,2048]{1,0:T(8,128)}) %all-reduce.15.cloned.1.call-update) | async-done | bytes 4194320 | tf_op jit(solution)/shard_map/psum | solution.py:220
  881.7 4.5 fusion.61
  886.2 24.1 %all-reduce.3 = (f32[2048]{0:T(1024)S(1)}, f32[2048]{0:T(1024)S(1)}) all-reduce(f32[2048]{0:T(1024)S(1)} %get-tuple-element.169, f32[2048]{0:T(1024)S(1)} %get-tuple-element.167), channel_id=9, replica_groups=mesh['fsdp'=4,'ctx'=2,'tp'=4] {'fsdp','ctx'}, use_global_device_ids=true, to_apply=%region_23.24.clone | all-reduce | flops 4096 | bytes 32768
  911.6 7.8 fusion.58
  920.3 39.8 %reduce-scatter.10.cloned.1.call-done = f32[256,128]{1,0:T(8,128)} async-done(((f32[2048,128]{1,0:T(8,128)}), f32[256,128]{1,0:T(8,128)}) %reduce-scatter.10.cloned.1.call-update) | async-done | bytes 131088 | tf_op jit(solution)/shard_map/reduce_scatter | solution.py:225
  960.1 54.9 %reduce-scatter.14.cloned.1.call-done = f32[512,256]{1,0:T(8,128)} async-done(((f32[512,2048]{1,0:T(8,128)}), f32[512,256]{1,0:T(8,128)}) %reduce-scatter.14.cloned.1.call-update) | async-done | bytes 524304 | tf_op jit(solution)/shard_map/reduce_scatter | solution.py:227
  1015.0 55.1 %reduce-scatter.8.cloned.1.call-done = f32[256,512]{1,0:T(8,128)} async-done(((f32[2048,512]{1,0:T(8,128)}), f32[256,512]{1,0:T(8,128)}) %reduce-scatter.8.cloned.1.call-update) | async-done | bytes 524304 | tf_op jit(solution)/shard_map/reduce_scatter | solution.py:224
  1070.1 120.2 %reduce-scatter.16.cloned.1.call-done = f32[256,2048]{1,0:T(8,128)} async-done(((f32[2048,2048]{1,0:T(8,128)}), f32[256,2048]{1,0:T(8,128)}) %reduce-scatter.16.cloned.1.call-update) | async-done | bytes 2097168 | tf_op jit(solution)/shard_map/reduce_scatter | solution.py:228
  1190.3 120.2 %reduce-scatter.18.cloned.1.call-done = f32[256,2048]{1,0:T(8,128)} async-done(((f32[2048,2048]{1,0:T(8,128)}), f32[256,2048]{1,0:T(8,128)}) %reduce-scatter.18.cloned.1.call-update) | async-done | bytes 2097168 | tf_op jit(solution)/shard_map/reduce_scatter | solution.py:229
  1310.5 120.0 %reduce-scatter.20.cloned.1.call-done = f32[2048,256]{1,0:T(8,128)} async-done(((f32[2048,2048]{1,0:T(8,128)}), f32[2048,256]{1,0:T(8,128)}) %reduce-scatter.20.cloned.1.call-update) | async-done | bytes 2097168 | tf_op jit(solution)/shard_map/reduce_scatter | solution.py:230
  (157 shorter events, 31.0 us)
Async XLA Ops:
  7.2 52.1 %all-gather.8.cloned.1.call-start = ((), (), s32[]{:S(2)}) async-start(), calls=%async_computation.7 | async-start | bytes 2359296 | tf_op jit(solution)/shard_map/all_gather | solution.py:133
  7.9 75.1 %all-gather.10.cloned.1.call-start = ((), (), s32[]{:S(2)}) async-start(), calls=%async_computation.8 | async-start | bytes 2359296 | tf_op jit(solution)/shard_map/all_gather | solution.py:136
  19.0 29.3 %copy-start.20 = (f32[8,1,256]{2,1,0:T(1,128)}, f32[8,1,256]{2,1,0:T(1,128)S(1)}, u32[]{:S(2)}) copy-start(f32[8,1,256]{2,1,0:T(1,128)S(1)} %convert_element_type.149) | copy-start | bytes 24580
  29.7 4.8 copy-start.7
  29.9 4.6 copy-start
  33.5 14.8 %copy-start.23 = (f32[512]{0:T(512)}, f32[512]{0:T(512)S(1)}, u32[]{:S(2)}) copy-start(f32[512]{0:T(512)S(1)} %get-tuple-element.236) | copy-start | bytes 6148
  34.5 31.6 %copy-start.13 = (f32[512,32]{0,1:T(8,128)}, f32[512,32]{0,1:T(8,128)S(1)}, u32[]{:S(2)}) copy-start(f32[512,32]{0,1:T(8,128)S(1)} %get-tuple-element.234) | copy-start | bytes 196612
  34.5 4.9 copy-start.22
  34.9 28.2 %copy-start.2 = (bf16[1,512,2048]{2,1,0:T(8,128)(2,1)}, bf16[1,512,2048]{2,1,0:T(8,128)(2,1)S(1)}, u32[]{:S(2)}) copy-start(bf16[1,512,2048]{2,1,0:T(8,128)(2,1)S(1)} %multiply_convert_fusion.5) | copy-start | bytes 6291460
  36.5 18.2 %collective-permute-start = (bf16[512,128]{0,1:T(8,128)(2,1)}, bf16[512,128]{0,1:T(8,128)(2,1)}, u32[]{:S(2)}, u32[]{:S(2)}) collective-permute-start(bf16[512,128]{0,1:T(8,128)(2,1)} %bitcast.31), channel_id=1, source_target_pairs={{0,4},{1,5},{2,6},{3,7},{8,12},{9,13},{10,14},{11,15},{16,20},{17,... | collective-permute-start | bytes 393224 | tf_op jit(solution)/shard_map/ppermute | solution.py:15
  48.3 3.2 copy-start.9
  48.8 1.4 copy-start.5
  51.5 4.2 collective-permute-start.1
  54.5 188.6 %all-reduce.9.cloned.1.call-start = ((), (), s32[]{:S(2)}) async-start(), calls=%async_computation.9 | async-start | bytes 8388608 | tf_op jit(solution)/shard_map/psum | solution.py:181
  67.9 2.4 copy-start.18
  74.3 2.4 copy-start.18
  87.9 1.8 copy-start.27
  87.9 210.1 %all-gather.12.cloned.1.call-start = ((), (), s32[]{:S(2)}) async-start(), calls=%async_computation.10 | async-start | bytes 9437184 | tf_op jit(solution)/shard_map/all_gather | solution.py:137
  88.5 265.6 %all-gather.14.cloned.1.call-start = ((), (), s32[]{:S(2)}) async-start(), calls=%async_computation.11 | async-start | bytes 9437184 | tf_op jit(solution)/shard_map/all_gather | solution.py:138
  89.1 322.6 %all-gather.16.cloned.1.call-start = ((), (), s32[]{:S(2)}) async-start(), calls=%async_computation.12 | async-start | bytes 9437184 | tf_op jit(solution)/shard_map/all_gather | solution.py:139
  89.7 507.0 %all-reduce.13.cloned.1.call-start = ((), (), s32[]{:S(2)}) async-start(), calls=%async_computation.14 | async-start | bytes 8388608 | tf_op jit(solution)/shard_map/psum | solution.py:194
  247.0 2.0 copy-start.1
  426.9 8.4 copy-start.30
  426.9 8.4 copy-start.26
  441.6 242.6 %all-reduce.11.cloned.1.call-start = ((), (), s32[]{:S(2)}) async-start(), calls=%async_computation.13 | async-start | bytes 4194304 | tf_op jit(solution)/shard_map/psum | solution.py:189
  451.4 430.3 %all-reduce.15.cloned.1.call-start = ((), (), s32[]{:S(2)}) async-start(), calls=%async_computation.15 | async-start | bytes 8388608 | tf_op jit(solution)/shard_map/psum | solution.py:220
  684.2 10.1 copy-start.12
  692.3 2.0 copy-start.4
  692.3 3.3 copy-start.19
  695.6 24.5 %copy-start.14 = (f32[512,32]{0,1:T(8,128)S(1)}, f32[512,32]{0,1:T(8,128)}, u32[]{:S(2)}) copy-start(f32[512,32]{0,1:T(8,128)} %copy-done.13) | copy-start | bytes 196612
  695.6 24.5 %copy-start.17 = (f32[512,32]{0,1:T(8,128)S(1)}, f32[512,32]{0,1:T(8,128)}, u32[]{:S(2)}) copy-start(f32[512,32]{0,1:T(8,128)} %get-tuple-element.232) | copy-start | bytes 196612
  697.0 3.3 copy-start.15
  701.8 1.0 copy-start.16
  707.3 3.3 copy-start.15
  712.0 1.0 copy-start.16
  716.1 5.5 copy-start.6
  717.3 6.5 collective-permute-start.3
  718.6 4.3 collective-permute-start.2
  721.6 1.5 copy-start.8
  722.9 1.0 copy-start.10
  726.8 3.6 copy-start.3
  726.8 193.6 %reduce-scatter.12.cloned.1.call-start = ((), (), s32[]{:S(2)}) async-start(), calls=%async_computation.18 | async-start | bytes 1179648 | tf_op jit(solution)/shard_map/reduce_scatter | solution.py:226
  730.3 229.8 %reduce-scatter.10.cloned.1.call-start = ((), (), s32[]{:S(2)}) async-start(), calls=%async_computation.17 | async-start | bytes 1179648 | tf_op jit(solution)/shard_map/reduce_scatter | solution.py:225
  732.2 282.8 %reduce-scatter.14.cloned.1.call-start = ((), (), s32[]{:S(2)}) async-start(), calls=%async_computation.19 | async-start | bytes 4718592 | tf_op jit(solution)/shard_map/reduce_scatter | solution.py:227
  737.9 332.2 %reduce-scatter.8.cloned.1.call-start = ((), (), s32[]{:S(2)}) async-start(), calls=%async_computation.16 | async-start | bytes 4718592 | tf_op jit(solution)/shard_map/reduce_scatter | solution.py:224
  741.3 1.6 copy-start.11
  741.3 449.0 %reduce-scatter.16.cloned.1.call-start = ((), (), s32[]{:S(2)}) async-start(), calls=%async_computation.20 | async-start | bytes 18874368 | tf_op jit(solution)/shard_map/reduce_scatter | solution.py:228
  752.6 557.9 %reduce-scatter.18.cloned.1.call-start = ((), (), s32[]{:S(2)}) async-start(), calls=%async_computation.21 | async-start | bytes 18874368 | tf_op jit(solution)/shard_map/reduce_scatter | solution.py:229
  762.6 1.6 copy-start.29
  762.6 668.0 %reduce-scatter.20.cloned.1.call-start = ((), (), s32[]{:S(2)}) async-start(), calls=%async_computation.22 | async-start | bytes 18874368 | tf_op jit(solution)/shard_map/reduce_scatter | solution.py:230
  774.5 0.7 copy-start.28
  774.5 107.2 %copy-start.21 = (f32[8,1,256]{2,1,0:T(1,128)S(1)}, f32[8,1,256]{2,1,0:T(1,128)}, u32[]{:S(2)}) copy-start(f32[8,1,256]{2,1,0:T(1,128)} %copy-done.20) | copy-start | bytes 24580
  774.6 107.2 %copy-start.24 = (f32[512]{0:T(512)S(1)}, f32[512]{0:T(512)}, u32[]{:S(2)}) copy-start(f32[512]{0:T(512)} %copy-done.23) | copy-start | bytes 6148
  776.4 135.1 %copy-start.25 = (f32[512]{0:T(512)S(1)}, f32[512]{0:T(512)}, u32[]{:S(2)}) copy-start(f32[512]{0:T(512)} %get-tuple-element.235) | copy-start | bytes 6148
Sparse Core Ops, SparseCore 0:
  9.9 31.1 all-gather.7
  54.6 28.3 all-gather.9
  88.0 154.9 all-reduce.8
  244.8 53.2 all-gather.11
  299.8 54.2 all-gather.13
  355.8 55.8 all-gather.15
  441.7 154.9 all-reduce.12
  599.0 85.0 all-reduce.10
  726.9 154.7 all-reduce.14
  885.3 34.9 reduce-scatter.11
  924.1 35.9 reduce-scatter.9
  963.9 51.0 reduce-scatter.13
  1018.9 51.1 reduce-scatter.7
  1074.1 116.1 reduce-scatter.15
  1194.3 116.1 reduce-scatter.17
  1314.5 115.9 reduce-scatter.19
where the time goes:
time: 1450 us; the launch traced here: 1440 us
  waiting for transfers between devices  1130 us (78%)
  matrix products  149 us (10%)
  blocking collectives  63.1 us (4%)
  other arithmetic  46.2 us (3%)
  local copies, waits for them, and re-layouts  19 us (1%)
  between operations  15.6 us (1%)
    psum x1, waiting for transfers between devices, body(): d_hnorm = lax.psum(dotf(d_gate, wg.T) + dotf(d_up, wu.T), 'tp')  145 us
    psum x1, waiting for transfers between devices, body(): hidden = rows + lax.psum(dotf(attn_flat, wo), 'tp')  144 us
    dot_general x21, matrix products, dotf(): return jnp.dot(left, right, preferred_element_type=jnp.float32)  121 us
    reduce_scatter x1, waiting for transfers between devices, body(): lax.psum_scatter(dotf(hnorm.T, d_gate), ('fsdp', 'ctx'), scatter_dimensio...  120 us
    reduce_scatter x1, waiting for transfers between devices, body(): lax.psum_scatter(dotf(hnorm.T, d_up), ('fsdp', 'ctx'), scatter_dimension=...  120 us
    reduce_scatter x1, waiting for transfers between devices, body(): lax.psum_scatter(dotf(inner.T, cot_b), ('fsdp', 'ctx'), scatter_dimension...  120 us
    psum x1, waiting for transfers between devices, body(): lax.psum(dotf(dq_b, wq.T) + dotf(dk_b, wk.T) + dotf(dv_b, wv.T), 'tp')  105 us
    psum x1, waiting for transfers between devices, body(): lax.psum(dotf(inner, wd).astype(jnp.bfloat16), 'tp').astype(jnp.float32)  83 us
  transfers between devices with their start and end apart: 20, of which 15 were waited for; matrix products, arithmetic and copies ran while one was open for 9% of the time, Pallas kernels for 0%

commit v1 on v0

--- a/solution.py
+++ b/solution.py
@@ -7,6 +7,17 @@
 EPS = 1e-05
 BASE = 500000.0
 NEG = -1e30
+
+
+def gather_around(x, axis, dim):
+    ways = lax.axis_size(axis)
+    pieces = [x]
+    for far in range(1, ways):
+        pieces.append(
+            lax.ppermute(pieces[far - 1], axis, [(d, (d - 1) % ways) for d in range(ways)])
+        )
+    line = jnp.concatenate(pieces, axis=dim)
+    return jnp.roll(line, lax.axis_index(axis) * x.shape[dim], axis=dim)
 
 
 def shifted(shard, axis, by):
@@ -135,7 +146,7 @@
         lax.all_gather(w_value, ("fsdp", "ctx"), axis=0, tiled=True),
         lax.all_gather(w_output, ("fsdp", "ctx"), axis=1, tiled=True),
         lax.all_gather(w_gate, ("fsdp", "ctx"), axis=0, tiled=True),
-        lax.all_gather(w_up, ("fsdp", "ctx"), axis=0, tiled=True),
+        gather_around(w_up, ("fsdp", "ctx"), 0),
         lax.all_gather(w_down, ("fsdp", "ctx"), axis=1, tiled=True),
         lax.all_gather(attn_gain, ("fsdp", "ctx"), axis=0, tiled=True),
         lax.all_gather(ffn_gain, ("fsdp", "ctx"), axis=0, tiled=True),

time: 1450 us -> 1400 us (0.966)
  waiting for transfers between devices: 1130 us -> 1040 us
  local copies, waits for them, and re-layouts: 19 us -> 46.4 us
  starting transfers between devices: 9.73 us -> 27.5 us
    psum x1, waiting for transfers between devices: 144 us -> 26 us  [body(): hidden = rows + lax.psum(dotf(attn_flat, wo), 'tp')]
    ppermute x0 -> x7, waiting for transfers between devices: none -> 66.3 us  [gather_around(): lax.ppermute(pieces[far - 1], axis, [(d, (d - 1) % ways) for d in range(w...]
    all_gather x1 -> x0, waiting for transfers between devices: 45.5 us -> none  [body(): lax.all_gather(w_up, ('fsdp', 'ctx'), axis=0, tiled=True)]
    unnamed x61 -> x98, local copies, waits for them, and re-layouts: 11.5 us -> 37.9 us
    ppermute x0 -> x7, starting transfers between devices: none -> 17.6 us  [gather_around(): lax.ppermute(pieces[far - 1], axis, [(d, (d - 1) % ways) for d in range(w...]
  transfers between devices with their start and end apart: 20 -> 26, of which waited for: 15 -> 20; matrix products, arithmetic and copies ran while one was open for 9% -> 11% of each run, Pallas kernels for 0% -> 0%
where the time goes in v1:
time: 1400 us; the launch traced here: 1390 us
  waiting for transfers between devices  1040 us (74%)
  matrix products  149 us (11%)
  blocking collectives  70.3 us (5%)
  local copies, waits for them, and re-layouts  46.4 us (3%)
  other arithmetic  46.2 us (3%)
  starting transfers between devices  27.5 us (2%)
  between operations  15.6 us (1%)
    psum x1, waiting for transfers between devices, body(): d_hnorm = lax.psum(dotf(d_gate, wg.T) + dotf(d_up, wu.T), 'tp')  145 us
    dot_general x21, matrix products, dotf(): return jnp.dot(left, right, preferred_element_type=jnp.float32)  121 us
    reduce_scatter x1, waiting for transfers between devices, body(): lax.psum_scatter(dotf(hnorm.T, d_gate), ('fsdp', 'ctx'), scatter_dimensio...  120 us
    reduce_scatter x1, waiting for transfers between devices, body(): lax.psum_scatter(dotf(hnorm.T, d_up), ('fsdp', 'ctx'), scatter_dimension=...  120 us
    reduce_scatter x1, waiting for transfers between devices, body(): lax.psum_scatter(dotf(inner.T, cot_b), ('fsdp', 'ctx'), scatter_dimension...  120 us
    psum x1, waiting for transfers between devices, body(): lax.psum(dotf(dq_b, wq.T) + dotf(dk_b, wk.T) + dotf(dv_b, wv.T), 'tp')  105 us
    psum x1, waiting for transfers between devices, body(): lax.psum(dotf(inner, wd).astype(jnp.bfloat16), 'tp').astype(jnp.float32)  83 us
    ppermute x7, waiting for transfers between devices, gather_around(): lax.ppermute(pieces[far - 1], axis, [(d, (d - 1) % ways) for d in range(w...  66.3 us
  transfers between devices with their start and end apart: 26, of which 20 were waited for; matrix products, arithmetic and copies ran while one was open for 11% of the time, Pallas kernels for 0%

profile of v1, /device:TPU:0, one launch (start us, length us, event | category | flops | bytes accessed | tf_op | source)
XLA Modules:
  0.0 1392.5 jit_solution(15430772283138234099)
XLA Ops:
  8.6 10.4 all-gather
  19.0 10.7 all_gather.26
  30.0 3.0 fusion.56
  36.5 2.9 collective-permute-start
  39.4 8.9 all_gather.27
  51.5 2.9 collective-permute-start.1
  59.2 3.9 copy.28
  63.1 2.9 fusion.72
  66.2 12.7 while.10
  67.9 2.3 exponential_reduce_fusion.2
  74.2 2.3 exponential_reduce_fusion.2
  78.9 4.0 all-gather.9.cloned.1.call-done
  83.0 4.9 fusion.96
  90.7 12.3 collective-permute-done.2
  104.0 3.2 collective-permute-start.3
  107.2 12.3 collective-permute-done.3
  120.5 3.2 collective-permute-start.4
  123.7 12.3 collective-permute-done.4
  137.0 3.2 collective-permute-start.5
  140.2 12.3 collective-permute-done.5
  153.5 3.2 collective-permute-start.6
  156.7 12.3 collective-permute-done.6
  169.0 2.9 collective-permute-start.7
  171.9 16.3 %all-gather.1 = bf16[8,1,256]{2,1,0:T(2,128)(2,1)S(1)} all-gather(bf16[1,1,256]{2,1,0:T(2,128)(2,1)S(1)} %reshape.299), channel_id=1, replica_groups=mesh['fsdp'=4,'ctx'=2,'tp'=4] {'fsdp','ctx'}, dimensions={0}, use_global_device_ids=true | all-gather | bytes 4608 | tf_op jit(solution)/shard_map/all_gather | solution.py:152
  189.3 2.6 constant_dynamic-update-slice_fusion.14
  195.6 2.4 constant_dynamic-update-slice_fusion.10
  200.3 4.7 collective-permute-done.8
  213.7 2.3 constant_dynamic-update-slice_fusion.1
  217.1 26.0 %all-reduce.9.cloned.1.call-done = f32[512,2048]{1,0:T(8,128)} async-done(((f32[512,2048]{1,0:T(8,128)}), f32[512,2048]{1,0:T(8,128)}) %all-reduce.9.cloned.1.call-update) | async-done | bytes 4194320 | tf_op jit(solution)/shard_map/psum | solution.py:192
  243.0 4.0 multiply_reduce_fusion.2
  250.8 47.2 %all-gather.11.cloned.1.call-done = bf16[2048,2048]{1,0:T(8,128)(2,1)} async-done(((bf16[256,2048]{1,0:T(8,128)(2,1)}), bf16[2048,2048]{1,0:T(8,128)(2,1)}) %all-gather.11.cloned.1.call-update) | async-done | bytes 8388624 | tf_op jit(solution)/shard_map/all_gather | solution.py:148
  298.0 10.6 fusion.97
  308.6 47.0 %all-gather.13.cloned.1.call-done = bf16[2048,2048]{1,0:T(8,128)(2,1)} async-done(((bf16[2048,256]{1,0:T(8,128)(2,1)}), bf16[2048,2048]{1,0:T(8,128)(2,1)}) %all-gather.13.cloned.1.call-update) | async-done | bytes 8388624 | tf_op jit(solution)/shard_map/all_gather | solution.py:150
  355.7 11.3 fusion.90
  367.0 12.6 multiply_convert_fusion.1
  379.7 6.9 fusion.98
  386.6 9.8 fusion.67
  396.4 9.8 convolution_convert_fusion
  406.5 145.0 %all-reduce.13.cloned.1.call-done = f32[512,2048]{1,0:T(8,128)} async-done(((f32[512,2048]{1,0:T(8,128)}), f32[512,2048]{1,0:T(8,128)}) %all-reduce.13.cloned.1.call-update) | async-done | bytes 4194320 | tf_op jit(solution)/shard_map/psum | solution.py:205
  551.6 4.5 multiply_reduce_fusion
  556.1 83.0 %all-reduce.11.cloned.1.call-done = bf16[512,2048]{1,0:T(8,128)(2,1)} async-done(((bf16[512,2048]{1,0:T(8,128)(2,1)}), bf16[512,2048]{1,0:T(8,128)(2,1)}) %all-reduce.11.cloned.1.call-update) | async-done | bytes 2097168 | tf_op jit(solution)/shard_map/psum | solution.py:200
  639.1 8.1 bitcast_add_fusion
  650.5 20.4 %while.27 = (s32[]{:T(128)}, f32[2,4,512,64]{2,3,1,0:T(8,128)}, f32[2,1024,64]{1,2,0:T(8,128)S(1)}, f32[2,1024,64]{1,2,0:T(8,128)}, pred[512,1024]{1,0:T(8,128)(...) while((s32[]{:T(128)}, f32[2,4,512,64]{2,3,1,0:T(8,128)}, ...), condition=%wide.region_12.13_spmd, body=%wide.region_10.12_spmd.sunk | while | flops 1365768192 | bytes 50255028 | solution.py:123
  651.9 3.3 multiply_convert_fusion.7
  657.6 3.1 fusion.177
  662.2 3.3 multiply_convert_fusion.7
  667.8 3.1 fusion.177
  678.8 2.8 add_add_fusion
  681.7 3.5 fusion.101
  687.0 5.7 fusion.80
  692.8 3.3 fusion.76
  697.7 9.8 fusion.102
  707.6 9.9 fusion.103
  719.1 10.4 fusion.92
  731.4 105.1 %all-reduce.15.cloned.1.call-done = f32[512,2048]{1,0:T(8,128)} async-done(((f32[512,2048]{1,0:T(8,128)}), f32[512,2048]{1,0:T(8,128)}) %all-reduce.15.cloned.1.call-update) | async-done | bytes 4194320 | tf_op jit(solution)/shard_map/psum | solution.py:231
  836.5 4.5 fusion.65
  841.0 24.1 %all-reduce.3 = (f32[2048]{0:T(1024)S(1)}, f32[2048]{0:T(1024)S(1)}) all-reduce(f32[2048]{0:T(1024)S(1)} %get-tuple-element.169, f32[2048]{0:T(1024)S(1)} %get-tuple-element.167), channel_id=9, replica_groups=mesh['fsdp'=4,'ctx'=2,'tp'=4] {'fsdp','ctx'}, use_global_device_ids=true, to_apply=%region_23.24.clone | all-reduce | flops 4096 | bytes 32768
  866.4 7.8 fusion.62
  875.3 39.6 %reduce-scatter.10.cloned.1.call-done = f32[256,128]{1,0:T(8,128)} async-done(((f32[2048,128]{1,0:T(8,128)}), f32[256,128]{1,0:T(8,128)}) %reduce-scatter.10.cloned.1.call-update) | async-done | bytes 131088 | tf_op jit(solution)/shard_map/reduce_scatter | solution.py:236
  914.9 55.0 %reduce-scatter.14.cloned.1.call-done = f32[512,256]{1,0:T(8,128)} async-done(((f32[512,2048]{1,0:T(8,128)}), f32[512,256]{1,0:T(8,128)}) %reduce-scatter.14.cloned.1.call-update) | async-done | bytes 524304 | tf_op jit(solution)/shard_map/reduce_scatter | solution.py:238
  969.9 55.0 %reduce-scatter.8.cloned.1.call-done = f32[256,512]{1,0:T(8,128)} async-done(((f32[2048,512]{1,0:T(8,128)}), f32[256,512]{1,0:T(8,128)}) %reduce-scatter.8.cloned.1.call-update) | async-done | bytes 524304 | tf_op jit(solution)/shard_map/reduce_scatter | solution.py:235
  1024.9 120.4 %reduce-scatter.16.cloned.1.call-done = f32[256,2048]{1,0:T(8,128)} async-done(((f32[2048,2048]{1,0:T(8,128)}), f32[256,2048]{1,0:T(8,128)}) %reduce-scatter.16.cloned.1.call-update) | async-done | bytes 2097168 | tf_op jit(solution)/shard_map/reduce_scatter | solution.py:239
  1145.3 120.2 %reduce-scatter.18.cloned.1.call-done = f32[256,2048]{1,0:T(8,128)} async-done(((f32[2048,2048]{1,0:T(8,128)}), f32[256,2048]{1,0:T(8,128)}) %reduce-scatter.18.cloned.1.call-update) | async-done | bytes 2097168 | tf_op jit(solution)/shard_map/reduce_scatter | solution.py:240
  1265.5 120.0 %reduce-scatter.20.cloned.1.call-done = f32[2048,256]{1,0:T(8,128)} async-done(((f32[2048,2048]{1,0:T(8,128)}), f32[2048,256]{1,0:T(8,128)}) %reduce-scatter.20.cloned.1.call-update) | async-done | bytes 2097168 | tf_op jit(solution)/shard_map/reduce_scatter | solution.py:241
  (207 shorter events, 76.1 us)
Async XLA Ops:
  7.2 52.0 %all-gather.7.cloned.1.call-start = ((), (), s32[]{:S(2)}) async-start(), calls=%async_computation.7 | async-start | bytes 2359296 | tf_op jit(solution)/shard_map/all_gather | solution.py:144
  7.9 75.1 %all-gather.9.cloned.1.call-start = ((), (), s32[]{:S(2)}) async-start(), calls=%async_computation.8 | async-start | bytes 2359296 | tf_op jit(solution)/shard_map/all_gather | solution.py:147
  19.0 29.3 %copy-start.30 = (f32[8,1,256]{2,1,0:T(1,128)}, f32[8,1,256]{2,1,0:T(1,128)S(1)}, u32[]{:S(2)}) copy-start(f32[8,1,256]{2,1,0:T(1,128)S(1)} %convert_element_type.149) | copy-start | bytes 24580
  29.7 4.8 copy-start.7
  29.9 4.6 copy-start
  33.5 14.8 %copy-start.33 = (f32[512]{0:T(512)}, f32[512]{0:T(512)S(1)}, u32[]{:S(2)}) copy-start(f32[512]{0:T(512)S(1)} %get-tuple-element.236) | copy-start | bytes 6148
  34.5 31.5 %copy-start.23 = (f32[512,32]{0,1:T(8,128)}, f32[512,32]{0,1:T(8,128)S(1)}, u32[]{:S(2)}) copy-start(f32[512,32]{0,1:T(8,128)S(1)} %get-tuple-element.234) | copy-start | bytes 196612
  34.5 4.9 copy-start.32
  34.9 28.2 %copy-start.2 = (bf16[1,512,2048]{2,1,0:T(8,128)(2,1)}, bf16[1,512,2048]{2,1,0:T(8,128)(2,1)S(1)}, u32[]{:S(2)}) copy-start(bf16[1,512,2048]{2,1,0:T(8,128)(2,1)S(1)} %multiply_convert_fusion.5) | copy-start | bytes 6291460
  36.5 18.2 %collective-permute-start = (bf16[512,128]{0,1:T(8,128)(2,1)}, bf16[512,128]{0,1:T(8,128)(2,1)}, u32[]{:S(2)}, u32[]{:S(2)}) collective-permute-start(bf16[512,128]{0,1:T(8,128)(2,1)} %bitcast.31), channel_id=1, source_target_pairs={{0,4},{1,5},{2,6},{3,7},{8,12},{9,13},{10,14},{11,15},{16,20},{17,... | collective-permute-start | bytes 393224 | tf_op jit(solution)/shard_map/ppermute | solution.py:26
  48.3 3.2 copy-start.9
  48.8 1.4 copy-start.5
  51.5 4.2 collective-permute-start.1
  54.4 188.6 %all-reduce.9.cloned.1.call-start = ((), (), s32[]{:S(2)}) async-start(), calls=%async_computation.9 | async-start | bytes 8388608 | tf_op jit(solution)/shard_map/psum | solution.py:192
  67.9 2.4 copy-start.28
  74.2 2.4 copy-start.28
  87.9 1.5 copy-start.11
  87.9 84.0 %copy-start.36 = (bf16[256]{0:T(256)(128)(2,1)S(1)}, bf16[256]{0:T(256)(128)(2,1)}, u32[]{:S(2)}) copy-start(bf16[256]{0:T(256)(128)(2,1)} %param.25) | copy-start | bytes 1540
  87.9 210.1 %all-gather.11.cloned.1.call-start = ((), (), s32[]{:S(2)}) async-start(), calls=%async_computation.10 | async-start | bytes 9437184 | tf_op jit(solution)/shard_map/all_gather | solution.py:148
  88.5 267.2 %all-gather.13.cloned.1.call-start = ((), (), s32[]{:S(2)}) async-start(), calls=%async_computation.11 | async-start | bytes 9437184 | tf_op jit(solution)/shard_map/all_gather | solution.py:150
  89.1 462.5 %all-reduce.13.cloned.1.call-start = ((), (), s32[]{:S(2)}) async-start(), calls=%async_computation.13 | async-start | bytes 8388608 | tf_op jit(solution)/shard_map/psum | solution.py:205
  89.3 13.7 collective-permute-start.2
  104.0 15.5 %collective-permute-start.3 = (bf16[256,2048]{1,0:T(8,128)(2,1)S(1)}, bf16[256,2048]{1,0:T(8,128)(2,1)S(1)}, u32[]{:S(2)}, u32[]{:S(2)}) collective-permute-start(bf16[256,2048]{1,0:T(8,128)(2,1)S(1)} %collective-permute-done.2), channel_id=1, source_target_pairs={{0,28},{4,0},{8,4},{12,8},{16,12},{20,16},{24,20},{28,24},{1,29},{... | collective-permute-start | bytes 3145736 | tf_op jit(solution)/shard_map/ppermute | solution.py:17
  120.5 15.5 %collective-permute-start.4 = (bf16[256,2048]{1,0:T(8,128)(2,1)S(1)}, bf16[256,2048]{1,0:T(8,128)(2,1)S(1)}, u32[]{:S(2)}, u32[]{:S(2)}) collective-permute-start(bf16[256,2048]{1,0:T(8,128)(2,1)S(1)} %collective-permute-done.3), channel_id=1, source_target_pairs={{0,28},{4,0},{8,4},{12,8},{16,12},{20,16},{24,20},{28,24},{1,29},{... | collective-permute-start | bytes 3145736 | tf_op jit(solution)/shard_map/ppermute | solution.py:17
  137.0 15.5 %collective-permute-start.5 = (bf16[256,2048]{1,0:T(8,128)(2,1)S(1)}, bf16[256,2048]{1,0:T(8,128)(2,1)S(1)}, u32[]{:S(2)}, u32[]{:S(2)}) collective-permute-start(bf16[256,2048]{1,0:T(8,128)(2,1)S(1)} %collective-permute-done.4), channel_id=1, source_target_pairs={{0,28},{4,0},{8,4},{12,8},{16,12},{20,16},{24,20},{28,24},{1,29},{... | collective-permute-start | bytes 3145736 | tf_op jit(solution)/shard_map/ppermute | solution.py:17
  153.5 15.5 %collective-permute-start.6 = (bf16[256,2048]{1,0:T(8,128)(2,1)S(1)}, bf16[256,2048]{1,0:T(8,128)(2,1)}, u32[]{:S(2)}, u32[]{:S(2)}) collective-permute-start(bf16[256,2048]{1,0:T(8,128)(2,1)S(1)} %collective-permute-done.5), channel_id=1, source_target_pairs={{0,28},{4,0},{8,4},{12,8},{16,12},{20,16},{24,20},{28,24},{1,29},{... | collective-permute-start | bytes 3145736 | tf_op jit(solution)/shard_map/ppermute | solution.py:17
  169.0 22.9 %collective-permute-start.7 = (bf16[256,2048]{1,0:T(8,128)(2,1)}, bf16[256,2048]{1,0:T(8,128)(2,1)}, u32[]{:S(2)}, u32[]{:S(2)}) collective-permute-start(bf16[256,2048]{1,0:T(8,128)(2,1)} %collective-permute-done.6), channel_id=1, source_target_pairs={{0,28},{4,0},{8,4},{12,8},{16,12},{20,16},{24,20},{28,24},{1,29},{... | collective-permute-start | bytes 3145736 | tf_op jit(solution)/shard_map/ppermute | solution.py:17
  188.2 4.2 copy-start.15
  188.2 5.2 copy-start.17
  188.2 6.3 copy-start.19
  191.9 13.2 collective-permute-start.8
  195.6 11.6 copy-start.13
  247.0 2.0 copy-start.1
  355.7 11.3 copy-start.20
  355.7 24.0 %slice-start = ((s8[8388608]{0:T(1024)(128)(4,1)}), s8[4194304]{0:T(1024)(128)(4,1)S(1)}, s32[]{:S(2)}) async-start(s8[8388608]{0:T(1024)(128)(4,1)} %bitcast.266), calls=%async_computation.22 | async-start | bytes 8388608
  367.0 12.7 slice-start.1
  379.6 6.9 copy-start.39
  396.4 242.7 %all-reduce.11.cloned.1.call-start = ((), (), s32[]{:S(2)}) async-start(), calls=%async_computation.12 | async-start | bytes 4194304 | tf_op jit(solution)/shard_map/psum | solution.py:200
  406.3 430.2 %all-reduce.15.cloned.1.call-start = ((), (), s32[]{:S(2)}) async-start(), calls=%async_computation.14 | async-start | bytes 8388608 | tf_op jit(solution)/shard_map/psum | solution.py:231
  639.1 10.1 copy-start.22
  647.2 2.0 copy-start.4
  647.2 3.3 copy-start.29
  650.5 24.5 %copy-start.24 = (f32[512,32]{0,1:T(8,128)S(1)}, f32[512,32]{0,1:T(8,128)}, u32[]{:S(2)}) copy-start(f32[512,32]{0,1:T(8,128)} %copy-done.23) | copy-start | bytes 196612
  650.5 24.5 %copy-start.27 = (f32[512,32]{0,1:T(8,128)S(1)}, f32[512,32]{0,1:T(8,128)}, u32[]{:S(2)}) copy-start(f32[512,32]{0,1:T(8,128)} %get-tuple-element.232) | copy-start | bytes 196612
  651.9 3.3 copy-start.25
  662.1 3.3 copy-start.25
  670.9 5.5 copy-start.6
  672.1 6.5 collective-permute-start.10
  673.5 4.3 collective-permute-start.9
  676.4 1.5 copy-start.8
  677.8 1.0 copy-start.10
  681.6 3.6 copy-start.3
  681.6 193.7 %reduce-scatter.12.cloned.1.call-start = ((), (), s32[]{:S(2)}) async-start(), calls=%async_computation.17 | async-start | bytes 1179648 | tf_op jit(solution)/shard_map/reduce_scatter | solution.py:237
  685.2 229.7 %reduce-scatter.10.cloned.1.call-start = ((), (), s32[]{:S(2)}) async-start(), calls=%async_computation.16 | async-start | bytes 1179648 | tf_op jit(solution)/shard_map/reduce_scatter | solution.py:236
  687.0 283.0 %reduce-scatter.14.cloned.1.call-start = ((), (), s32[]{:S(2)}) async-start(), calls=%async_computation.18 | async-start | bytes 4718592 | tf_op jit(solution)/shard_map/reduce_scatter | solution.py:238
  692.7 332.2 %reduce-scatter.8.cloned.1.call-start = ((), (), s32[]{:S(2)}) async-start(), calls=%async_computation.15 | async-start | bytes 4718592 | tf_op jit(solution)/shard_map/reduce_scatter | solution.py:235
  696.1 1.6 copy-start.21
  696.1 449.1 %reduce-scatter.16.cloned.1.call-start = ((), (), s32[]{:S(2)}) async-start(), calls=%async_computation.19 | async-start | bytes 18874368 | tf_op jit(solution)/shard_map/reduce_scatter | solution.py:239
  707.5 558.0 %reduce-scatter.18.cloned.1.call-start = ((), (), s32[]{:S(2)}) async-start(), calls=%async_computation.20 | async-start | bytes 18874368 | tf_op jit(solution)/shard_map/reduce_scatter | solution.py:240
  717.5 1.6 copy-start.38
  717.5 668.0 %reduce-scatter.20.cloned.1.call-start = ((), (), s32[]{:S(2)}) async-start(), calls=%async_computation.21 | async-start | bytes 18874368 | tf_op jit(solution)/shard_map/reduce_scatter | solution.py:241
  729.5 107.0 %copy-start.31 = (f32[8,1,256]{2,1,0:T(1,128)S(1)}, f32[8,1,256]{2,1,0:T(1,128)}, u32[]{:S(2)}) copy-start(f32[8,1,256]{2,1,0:T(1,128)} %copy-done.30) | copy-start | bytes 24580
  729.5 107.0 %copy-start.34 = (f32[512]{0:T(512)S(1)}, f32[512]{0:T(512)}, u32[]{:S(2)}) copy-start(f32[512]{0:T(512)} %copy-done.33) | copy-start | bytes 6148
  731.4 135.0 %copy-start.35 = (f32[512]{0:T(512)S(1)}, f32[512]{0:T(512)}, u32[]{:S(2)}) copy-start(f32[512]{0:T(512)} %get-tuple-element.235) | copy-start | bytes 6148
  (7 other events, 6.5 us)
Sparse Core Ops, SparseCore 0:
  9.9 31.1 all-gather.6
  54.6 28.3 all-gather.8
  88.0 154.9 all-reduce.8
  244.8 53.2 all-gather.10
  299.8 55.8 all-gather.12
  396.5 155.0 all-reduce.12
  553.9 85.0 all-reduce.10
  681.7 154.7 all-reduce.14
  840.3 34.9 reduce-scatter.11
  878.9 35.9 reduce-scatter.9
  918.8 51.0 reduce-scatter.13
  973.7 51.1 reduce-scatter.7
  1029.0 116.1 reduce-scatter.15
  1149.3 116.1 reduce-scatter.17
  1269.5 115.9 reduce-scatter.19
